TPU v7x, 32 devices: a whole 2x2x4 slice. The times are simulated.
32 devices in a mesh: ctx: 16 (over z, y, x), fsdp: 2 (over core).
Axes of the slice: x: 2, y: 2, z: 4, core: 2. Of those that a mesh axis runs over, the one named last changes fastest.
Arguments:
- inputs: bfloat16 [2, 2048, 1024], P('fsdp', 'ctx'), may hold values from -48 to 48
- cotangent: bfloat16 [2, 2048, 1024], P('fsdp', 'ctx'), may hold values from -6 to 6
- doc_lengths: int32 [2, 8], P('fsdp'), may hold values from 1 to 1024, 2048 in all within a row
- qkv_weight: bfloat16 [1024, 3072], P('fsdp'), may hold values from -0.1875 to 0.1875
- out_weight: bfloat16 [1024, 1024], P('fsdp'), may hold values from -0.1875 to 0.1875
- fc1_weight: bfloat16 [1024, 4096], P('fsdp'), may hold values from -0.1875 to 0.1875
- fc2_weight: bfloat16 [4096, 1024], P('fsdp'), may hold values from -0.09375 to 0.09375
- norm_gain: bfloat16 [3, 1024], P(None, 'fsdp'), may hold values from 0.099609375 to 1.8984375
- norm_bias: bfloat16 [3, 1024], P(None, 'fsdp'), may hold values from -1.5 to 1.5
- mid_gain: bfloat16 [4096], P('fsdp'), may hold values from 0.099609375 to 1.8984375
- mid_bias: bfloat16 [4096], P('fsdp'), may hold values from -1.5 to 1.5
- head_scale: bfloat16 [16], P('fsdp'), may hold values from 0.5 to 2
Outputs:
- output: bfloat16 [2, 2048, 1024], P('fsdp', 'ctx')
- input_grad: bfloat16 [2, 2048, 1024], P('fsdp', 'ctx')
- qkv_grad: float32 [1024, 3072], P('fsdp')
- out_grad: float32 [1024, 1024], P('fsdp')
- fc1_grad: float32 [1024, 4096], P('fsdp')
- fc2_grad: float32 [4096, 1024], P('fsdp')
- gain_grad: float32 [3, 1024], P(None, 'fsdp')
- bias_grad: float32 [3, 1024], P(None, 'fsdp')
- mid_gain_grad: float32 [4096], P('fsdp')
- mid_bias_grad: float32 [4096], P('fsdp')
- scale_grad: float32 [16], P('fsdp')
- rms_values: float32 [3], replicated
Inputs may be any that keep to these rules, and one draw needn't show every extreme that they name: `doc_lengths`: each row holds 8 document lengths that sum to 2048; the longest is 1024.
All inputs are finite; a program needn't handle non-finite values.
Results may differ from a plain program's by a relative error of at most 0.022.
Values may be sent and summed in bfloat16 or wider, within the bound.
No kernel may reach another device: no remote copies, remote signals or barrier semaphores. Data moves between devices by JAX's collectives and lax.ppermute only.
A program may use at most 320 MiB of HBM per device.

v0:
```python
from functools import partial
import math
import jax
import jax.numpy as jnp
from jax import lax
from jax.sharding import PartitionSpec as P

HEADS = 16
HEAD_DIM = 64
epsilon = 1e-05
masked_value = -1e30


def stored_positions(first_row, n_rows, half_rows, groups):
    offsets = first_row + jnp.arange(n_rows, dtype=jnp.int32)
    halves = offsets // half_rows
    paired = halves // 2
    placed = jnp.where(halves % 2 == 0, paired, 2 * groups - 1 - paired)
    return placed * half_rows + offsets % half_rows


def doc_floor(positions, starts):
    begun_mask = starts[None, :] <= positions[:, None]
    return jnp.max(jnp.where(begun_mask, starts[None, :], 0), axis=1)


def allowed_mask(query_pos, query_floor, key_pos):
    return (key_pos[None, :] <= query_pos[:, None]) & (key_pos[None, :] >= query_floor[:, None])


def normalize(values):
    centered = values - jnp.mean(values, axis=-1, keepdims=True)
    inverse = lax.rsqrt(jnp.mean(centered * centered, axis=-1, keepdims=True) + epsilon)
    return (centered * inverse, inverse)


def norm_backward(grad_out, normed, inverse, gain_vec):
    grad_normed = grad_out * gain_vec
    grad_in = inverse * (
        grad_normed
        - jnp.mean(grad_normed, axis=-1, keepdims=True)
        - normed * jnp.mean(grad_normed * normed, axis=-1, keepdims=True)
    )
    return (grad_in, jnp.sum(grad_out * normed, axis=0), jnp.sum(grad_out, axis=0))


def split_heads(rows_array, model_width):
    n_rows = rows_array.shape[0]
    return (
        rows_array[:, :model_width].reshape(n_rows, HEADS, HEAD_DIM),
        rows_array[:, model_width:].reshape(n_rows, HEADS, HEAD_DIM),
    )


def block_grads(query_heads, dout_heads, log_total, delta_rows, key_heads, value_heads, allowed):
    scores = jnp.einsum(
        "qhe,khe->qhk", query_heads, key_heads, preferred_element_type=jnp.float32
    ) * HEAD_DIM ** (-0.5)
    p_block = jnp.where(allowed[:, None, :], jnp.exp(scores - log_total[:, :, None]), 0.0)
    grad_probs = jnp.einsum(
        "qhe,khe->qhk", dout_heads, value_heads, preferred_element_type=jnp.float32
    )
    grad_scores = (p_block * (grad_probs - delta_rows[:, :, None])).astype(jnp.bfloat16)
    return (grad_scores, p_block.astype(jnp.bfloat16))


def local(
    inputs,
    cotangent,
    doc_lengths,
    qkv_weight,
    out_weight,
    fc1_weight,
    fc2_weight,
    norm_gain,
    norm_bias,
    mid_gain,
    mid_bias,
    head_scale,
):
    groups = lax.axis_size("ctx")
    member = lax.axis_index("ctx")
    x_local = inputs[0].astype(jnp.float32)
    tok_rows, model_width = x_local.shape
    half_rows = tok_rows // 2
    stream_rows = tok_rows * groups
    score_scale = HEAD_DIM ** (-0.5)
    (
        qkv_full,
        out_full,
        fc1_full,
        fc2_full,
        gain_full,
        bias_full,
        mid_gain_full,
        mid_bias_full,
        scale_full,
    ) = (
        lax.all_gather(qkv_weight, "fsdp", axis=0, tiled=True),
        lax.all_gather(out_weight, "fsdp", axis=0, tiled=True),
        lax.all_gather(fc1_weight, "fsdp", axis=0, tiled=True),
        lax.all_gather(fc2_weight, "fsdp", axis=0, tiled=True),
        lax.all_gather(norm_gain, "fsdp", axis=1, tiled=True),
        lax.all_gather(norm_bias, "fsdp", axis=1, tiled=True),
        lax.all_gather(mid_gain, "fsdp", axis=0, tiled=True),
        lax.all_gather(mid_bias, "fsdp", axis=0, tiled=True),
        lax.all_gather(head_scale, "fsdp", axis=0, tiled=True),
    )
    norm_gains = gain_full.astype(jnp.float32)
    norm_biases = bias_full.astype(jnp.float32)
    mid_gains = mid_gain_full.astype(jnp.float32)
    mid_biases = mid_bias_full.astype(jnp.float32)
    head_scales = scale_full.astype(jnp.float32)
    lengths_row = doc_lengths[0]
    starts = jnp.cumsum(lengths_row) - lengths_row
    my_pos = stored_positions(member * tok_rows, tok_rows, half_rows, groups)
    my_floor = doc_floor(my_pos, starts)
    norm_one, inv_one = normalize(x_local)
    normed_one = (norm_one * norm_gains[0] + norm_biases[0]).astype(jnp.bfloat16)
    project = jnp.dot(normed_one, qkv_full, preferred_element_type=jnp.float32).astype(jnp.bfloat16)
    queries = project[:, :model_width].reshape(tok_rows, HEADS, HEAD_DIM)
    keys_values = project[:, model_width:]
    start_state = (
        jnp.zeros((tok_rows, HEADS, HEAD_DIM), jnp.float32),
        jnp.full((tok_rows, HEADS), masked_value, jnp.float32),
        jnp.zeros((tok_rows, HEADS), jnp.float32),
    )
    running = start_state
    fetched = lax.all_gather(keys_values, "ctx", axis=0, tiled=True)
    n_rows = fetched.shape[0]
    sub_rows = math.gcd(n_rows, 1024)
    fetched_blocks = fetched.reshape(n_rows // sub_rows, sub_rows, 2 * model_width)
    block_firsts = sub_rows * jnp.arange(n_rows // sub_rows, dtype=jnp.int32)

    def attend_block(state_now, scanned):
        out_sum, row_max, row_sum = state_now
        key_block, block_first = scanned
        key_heads, value_heads = split_heads(key_block, model_width)
        key_pos = stored_positions(block_first, sub_rows, half_rows, groups)
        usable = allowed_mask(my_pos, my_floor, key_pos)[:, None, :]
        scores = (
            jnp.einsum("qhe,khe->qhk", queries, key_heads, preferred_element_type=jnp.float32)
            * score_scale
        )
        new_max = jnp.maximum(row_max, jnp.max(jnp.where(usable, scores, masked_value), axis=-1))
        p_block = jnp.where(usable, jnp.exp(scores - new_max[:, :, None]), 0.0)
        rescale = jnp.exp(row_max - new_max)
        row_sum = row_sum * rescale + jnp.sum(p_block, axis=-1)
        out_sum = out_sum * rescale[:, :, None] + jnp.einsum(
            "qhk,khe->qhe",
            p_block.astype(jnp.bfloat16),
            value_heads,
            preferred_element_type=jnp.float32,
        )
        return ((out_sum, new_max, row_sum), None)

    running, unused_out = lax.scan(attend_block, running, (fetched_blocks, block_firsts))
    out_sum, row_max, row_sum = running
    attended = out_sum / row_sum[:, :, None]
    log_total = row_max + jnp.log(row_sum)
    scaled = (
        (attended * head_scales[None, :, None]).reshape(tok_rows, model_width).astype(jnp.bfloat16)
    )
    branch = jnp.dot(scaled, out_full, preferred_element_type=jnp.float32)
    norm_att, inv_att = normalize(branch)
    attn_out = norm_att * norm_gains[1] + norm_biases[1]
    middle = x_local + attn_out
    norm_two, inv_two = normalize(middle)
    normed_two = (norm_two * norm_gains[2] + norm_biases[2]).astype(jnp.bfloat16)
    hidden = jnp.dot(normed_two, fc1_full, preferred_element_type=jnp.float32)
    active, gelu_back = jax.vjp(partial(jax.nn.gelu, approximate=True), hidden)
    norm_mid, inv_mid = normalize(active)
    mixed_in = (norm_mid * mid_gains + mid_biases).astype(jnp.bfloat16)
    ffn_out = jnp.dot(mixed_in, fc2_full, preferred_element_type=jnp.float32)
    result = middle + ffn_out
    sq_sums = lax.psum(
        jnp.stack(
            [jnp.sum(result * result), jnp.sum(attn_out * attn_out), jnp.sum(ffn_out * ffn_out)]
        ),
        ("ctx", "fsdp"),
    )
    rms_values = jnp.sqrt(sq_sums / (stream_rows * lax.axis_size("fsdp") * model_width))
    grad_top = cotangent[0].astype(jnp.float32)
    grad_ffn = cotangent[0]
    fc2_grad = jnp.einsum("tf,td->fd", mixed_in, grad_ffn, preferred_element_type=jnp.float32)
    grad_mixed = jnp.einsum("td,fd->tf", grad_ffn, fc2_full, preferred_element_type=jnp.float32)
    grad_active, mid_gain_grad, mid_bias_grad = norm_backward(
        grad_mixed, norm_mid, inv_mid, mid_gains
    )
    grad_hidden = gelu_back(grad_active)[0].astype(jnp.bfloat16)
    fc1_grad = jnp.einsum("td,tf->df", normed_two, grad_hidden, preferred_element_type=jnp.float32)
    grad_two = jnp.einsum("tf,df->td", grad_hidden, fc1_full, preferred_element_type=jnp.float32)
    grad_mid_in, gain_two, bias_two = norm_backward(grad_two, norm_two, inv_two, norm_gains[2])
    grad_middle = grad_top + grad_mid_in
    grad_branch_f, gain_att, bias_att = norm_backward(grad_middle, norm_att, inv_att, norm_gains[1])
    grad_branch = grad_branch_f.astype(jnp.bfloat16)
    out_grad = jnp.einsum("ta,tb->ab", scaled, grad_branch, preferred_element_type=jnp.float32)
    grad_scaled = jnp.einsum(
        "tb,ab->ta", grad_branch, out_full, preferred_element_type=jnp.float32
    ).reshape(tok_rows, HEADS, HEAD_DIM)
    scale_grad = jnp.sum(grad_scaled * attended, axis=(0, 2))
    grad_att = (grad_scaled * head_scales[None, :, None]).astype(jnp.bfloat16)
    delta_rows = jnp.sum(grad_att.astype(jnp.float32) * attended, axis=-1)
    query_start = jnp.zeros((tok_rows, HEADS, HEAD_DIM), jnp.float32)
    every_kv = lax.all_gather(keys_values, "ctx", axis=0, tiled=True)
    running = query_start
    n_rows = every_kv.shape[0]
    query_sub_rows = math.gcd(n_rows, 1024)
    fetched_blocks = every_kv.reshape(n_rows // query_sub_rows, query_sub_rows, 2 * model_width)
    block_firsts = 0 + query_sub_rows * jnp.arange(n_rows // query_sub_rows, dtype=jnp.int32)

    def query_block(partial_sum, scanned):
        key_block, block_first = scanned
        key_heads, value_heads = split_heads(key_block, model_width)
        key_pos = stored_positions(block_first, query_sub_rows, half_rows, groups)
        allowed = allowed_mask(my_pos, my_floor, key_pos)
        grad_scores, unused_low = block_grads(
            queries, grad_att, log_total, delta_rows, key_heads, value_heads, allowed
        )
        return (
            partial_sum
            + jnp.einsum(
                "qhk,khe->qhe", grad_scores, key_heads, preferred_element_type=jnp.float32
            ),
            None,
        )

    running, unused_out = lax.scan(query_block, running, (fetched_blocks, block_firsts))
    n_rows = tok_rows * lax.axis_size("ctx")
    key_sub_rows = math.gcd(n_rows, 1024)

    def key_term(sub_first):
        key_block = lax.dynamic_slice_in_dim(every_kv, sub_first, key_sub_rows, 0)
        key_heads, value_heads = split_heads(key_block, model_width)
        key_pos = stored_positions(sub_first, key_sub_rows, half_rows, groups)
        allowed = allowed_mask(my_pos, my_floor, key_pos)
        grad_scores, low_probs = block_grads(
            queries, grad_att, log_total, delta_rows, key_heads, value_heads, allowed
        )
        grad_keys = (
            jnp.einsum("qhk,qhe->khe", grad_scores, queries, preferred_element_type=jnp.float32)
            * score_scale
        )
        grad_values = jnp.einsum(
            "qhk,qhe->khe", low_probs, grad_att, preferred_element_type=jnp.float32
        )
        return jnp.concatenate(
            [
                grad_keys.reshape(key_sub_rows, model_width),
                grad_values.reshape(key_sub_rows, model_width),
            ],
            axis=1,
        )

    sub_firsts = key_sub_rows * jnp.arange(n_rows // key_sub_rows, dtype=jnp.int32)
    kv_grad = lax.psum_scatter(
        lax.map(key_term, sub_firsts).reshape(n_rows, 2 * model_width),
        "ctx",
        scatter_dimension=0,
        tiled=True,
    )
    grad_queries = (running * score_scale).reshape(tok_rows, model_width)
    grad_project = jnp.concatenate([grad_queries, kv_grad], axis=1).astype(jnp.bfloat16)
    qkv_grad = jnp.einsum("td,tp->dp", normed_one, grad_project, preferred_element_type=jnp.float32)
    grad_one = jnp.einsum("tp,dp->td", grad_project, qkv_full, preferred_element_type=jnp.float32)
    grad_first, gain_one, bias_one = norm_backward(grad_one, norm_one, inv_one, norm_gains[0])
    input_grad = (grad_middle + grad_first).astype(jnp.bfloat16)[None]
    gain_grad = jnp.stack([gain_one, gain_att, gain_two])
    bias_grad = jnp.stack([bias_one, bias_att, bias_two])
    shard_grads = (
        lax.psum_scatter(
            qkv_grad.astype(jnp.bfloat16), "fsdp", scatter_dimension=0, tiled=True
        ).astype(jnp.float32),
        lax.psum_scatter(
            out_grad.astype(jnp.bfloat16), "fsdp", scatter_dimension=0, tiled=True
        ).astype(jnp.float32),
        lax.psum_scatter(
            fc1_grad.astype(jnp.bfloat16), "fsdp", scatter_dimension=0, tiled=True
        ).astype(jnp.float32),
        lax.psum_scatter(
            fc2_grad.astype(jnp.bfloat16), "fsdp", scatter_dimension=0, tiled=True
        ).astype(jnp.float32),
        lax.psum_scatter(
            gain_grad.astype(jnp.bfloat16), "fsdp", scatter_dimension=1, tiled=True
        ).astype(jnp.float32),
        lax.psum_scatter(
            bias_grad.astype(jnp.bfloat16), "fsdp", scatter_dimension=1, tiled=True
        ).astype(jnp.float32),
        lax.psum_scatter(
            mid_gain_grad.astype(jnp.bfloat16), "fsdp", scatter_dimension=0, tiled=True
        ).astype(jnp.float32),
        lax.psum_scatter(
            mid_bias_grad.astype(jnp.bfloat16), "fsdp", scatter_dimension=0, tiled=True
        ).astype(jnp.float32),
        lax.psum_scatter(
            scale_grad.astype(jnp.bfloat16), "fsdp", scatter_dimension=0, tiled=True
        ).astype(jnp.float32),
    )
    summed = lax.psum(
        (
            shard_grads[0],
            shard_grads[1],
            shard_grads[2],
            shard_grads[3],
            shard_grads[4],
            shard_grads[5],
            shard_grads[6],
            shard_grads[7],
            shard_grads[8],
        ),
        "ctx",
    )
    return (
        result.astype(jnp.bfloat16)[None],
        input_grad,
        summed[0],
        summed[1],
        summed[2],
        summed[3],
        summed[4],
        summed[5],
        summed[6],
        summed[7],
        summed[8],
        rms_values,
    )


def solution(mesh):
    placed = (
        P("fsdp", "ctx", None),
        P("fsdp", "ctx", None),
        P("fsdp", None),
        P("fsdp", None),
        P("fsdp", None),
        P("fsdp", None),
        P("fsdp", None),
        P(None, "fsdp"),
        P(None, "fsdp"),
        P("fsdp"),
        P("fsdp"),
        P("fsdp"),
    )
    return jax.shard_map(
        local,
        mesh=mesh,
        in_specs=placed,
        out_specs=(
            P("fsdp", "ctx", None),
            P("fsdp", "ctx", None),
            P("fsdp", None),
            P("fsdp", None),
            P("fsdp", None),
            P("fsdp", None),
            P(None, "fsdp"),
            P(None, "fsdp"),
            P("fsdp"),
            P("fsdp"),
            P("fsdp"),
            P(),
        ),
        check_vma=False,
    )
```

profile of v0, /device:TPU:26, one launch (start us, length us, event | category | flops | bytes accessed | tf_op | source)
XLA Modules:
  0.0 1870.3 jit_solution(4212419879417016194)
XLA Ops:
  12.1 15.5 all-gather.6.cloned.1.call-done
  43.0 100.6 %all-gather.8.cloned.1.call-done = bf16[2048,2048]{1,0:T(8,128)(2,1)} async-done(((bf16[128,2048]{1,0:T(8,128)(2,1)}), bf16[2048,2048]{1,0:T(8,128)(2,1)}) %all-gather.8.cloned.1.call-update) | async-done | bytes 8388624 | tf_op jit(solution)/shard_map/all_gather | solution.py:129
  143.6 12.0 copy.75
  155.7 40.6 %while.47 = (s32[]{:T(128)}, f32[128,16,64]{0,2,1:T(8,128)S(1)}, f32[128,16]{0,1:T(8,128)S(1)}, f32[128,16]{0,1:T(8,128)S(1)}, s32[2]{0:T(128)S(1)}, /*index=5*/...) while((s32[]{:T(128)}, f32[128,16,64]{0,2,1:T(8,128)S(1)}, ...), condition=%wide.region_7.8_spmd.clone, body=%wide.region_4.7_spmd.clone.sunk | while | flops 560786944 | bytes 81667752 | solution.py:157
  165.5 6.6 fusion.229
  185.8 6.3 fusion.229
  200.8 5.5 fusion.131
  207.5 6.7 multiply_reduce_fusion
  216.3 6.7 fusion.143
  230.1 116.8 %while.46 = (s32[]{:T(128)}, f32[2,1024,2048]{2,1,0:T(8,128)}, s32[2]{0:T(128)S(1)}, s32[128]{0:T(128)S(1)}, bf16[2048,2048]{1,0:T(8,128)(2,1)}, /*index=5*/bf16...) while((s32[]{:T(128)}, f32[2,1024,2048]{2,1,0:T(8,128)}, ...), condition=%wide.region_24.25_spmd.clone, body=%wide.region_23.24_spmd.clone.sunk | while | flops 1098302976 | bytes 123111664 | solution.py:257
  233.2 5.3 fusion.216
  242.4 6.3 fusion.217
  252.3 10.0 broadcast_multiply_fusion.14
  262.2 5.4 fusion.220
  271.9 9.1 copy.129
  281.0 7.7 constant_dynamic-update-slice_fusion.2
  291.4 5.3 fusion.216
  300.6 6.3 fusion.217
  310.5 10.0 broadcast_multiply_fusion.14
  320.4 5.4 fusion.220
  330.1 9.1 copy.129
  339.2 7.7 constant_dynamic-update-slice_fusion.2
  350.2 6.0 convolution_convert_fusion.1
  357.9 6.2 convolution_convert_fusion
  364.2 36.4 %while.48 = (s32[]{:T(128)}, f32[128,16,64]{0,2,1:T(8,128)S(1)}, bf16[2,1024,2048]{1,2,0:T(8,128)(2,1)}, s32[2]{0:T(128)S(1)}, s32[128]{0:T(128)S(1)}, /*index=5...) while((s32[]{:T(128)}, f32[128,16,64]{0,2,1:T(8,128)S(1)}, ...), condition=%wide.region_22.23_spmd.clone, body=%wide.region_21.22_spmd.clone.sunk | while | flops 818595328 | bytes 41707156 | solution.py:228
  374.6 7.8 fusion.242
  392.9 7.7 fusion.242
  400.9 299.6 %reduce-scatter.12.cloned.1.call-done = f32[128,2048]{1,0:T(8,128)} async-done(((f32[2048,2048]{1,0:T(8,128)}), f32[128,2048]{1,0:T(8,128)}) %reduce-scatter.12.cloned.1.call-update) | async-done | bytes 1048592 | tf_op jit(solution)/shard_map/reduce_scatter | solution.py:256
  717.0 38.6 %psum.79 = f32[3]{0:T(128)S(1)} all-reduce(f32[3]{0:T(128)S(1)} %pad_maximum_fusion.5), channel_id=1, replica_groups=mesh['ctx'=16,'fsdp'=2] {'ctx','fsdp'}, use_global_device_ids=true, to_apply=%region_58.59 | all-reduce | flops 3 | bytes 24 | tf_op jit(solution)/shard_map/psum | solution.py:176
  766.0 10.7 reduce-scatter.22.cloned.1.call-done
  777.7 17.9 reduce-scatter.14.cloned.1.call-done
  795.6 1067.7 %all-reduce.7 = (f32[512,3072]{1,0:T(8,128)}, f32[512,1024]{1,0:T(8,128)}, f32[512,4096]{1,0:T(8,128)}, f32[2048,1024]{1,0:T(8,128)}, f32[3,512]{1,0:T(4,128)}, ...) all-reduce(bf16[512,3072]{1,0:T(8,128)(2,1)} %reduce-scatter.14.clo, ...), channel_id=1, replica_groups=mesh['ctx'=16,'fsdp'=2] {'ctx'}, use_global_device_ids=true, to_apply=%region_29.30 | all-reduce | flops 6298632 | bytes 37800000 | tf_op jit(solution)/shard_map/psum | solution.py:299
  (291 shorter events, 138.4 us)
Async XLA Ops:
  7.2 20.4 %all-gather.6.cloned.1.call-start = ((), (), s32[]{:S(2)}) async-start(), calls=%async_computation.7 | async-start | bytes 9437184 | tf_op jit(solution)/shard_map/all_gather | solution.py:99
  7.9 135.7 %all-gather.8.cloned.1.call-start = ((), (), s32[]{:S(2)}) async-start(), calls=%async_computation.8 | async-start | bytes 8912896 | tf_op jit(solution)/shard_map/all_gather | solution.py:129
  11.8 19.7 %copy-start.35 = (f32[128]{0:T(128)}, f32[128]{0:T(128)S(1)}, u32[]{:S(2)}) copy-start(f32[128]{0:T(128)S(1)} %broadcast_multiply_fusion.12) | copy-start | bytes 1540
  12.0 214.6 %copy-start.29 = (f32[1,1024]{1,0:T(1,128)}, f32[1,1024]{1,0:T(1,128)S(1)}, u32[]{:S(2)}) copy-start(f32[1,1024]{1,0:T(1,128)S(1)} %get-tuple-element.858) | copy-start | bytes 12292
  12.1 188.7 %copy-start.33 = (f32[1,1024]{1,0:T(1,128)}, f32[1,1024]{1,0:T(1,128)S(1)}, u32[]{:S(2)}) copy-start(f32[1,1024]{1,0:T(1,128)S(1)} %get-tuple-element.861) | copy-start | bytes 12292
  32.3 164.1 %all-gather.10.cloned.1.call-start = ((), (), s32[]{:S(2)}) async-start(), calls=%async_computation.9 | async-start | bytes 3145728 | tf_op jit(solution)/shard_map/all_gather | solution.py:100
  33.1 167.7 %all-gather.12.cloned.1.call-start = ((), (), s32[]{:S(2)}) async-start(), calls=%async_computation.10 | async-start | bytes 12582912 | tf_op jit(solution)/shard_map/all_gather | solution.py:101
  33.7 173.6 %all-gather.14.cloned.1.call-start = ((), (), s32[]{:S(2)}) async-start(), calls=%async_computation.11 | async-start | bytes 12582912 | tf_op jit(solution)/shard_map/all_gather | solution.py:102
  34.3 666.2 %reduce-scatter.12.cloned.1.call-start = ((), (), s32[]{:S(2)}) async-start(), calls=%async_computation.12 | async-start | bytes 17825792 | tf_op jit(solution)/shard_map/reduce_scatter | solution.py:256
  40.4 182.7 %copy-start.27 = (f32[4096]{0:T(1024)}, f32[4096]{0:T(1024)S(1)}, u32[]{:S(2)}) copy-start(f32[4096]{0:T(1024)S(1)} %convert_element_type.149) | copy-start | bytes 49156
  42.7 180.4 %copy-start.31 = (f32[4096]{0:T(1024)}, f32[4096]{0:T(1024)S(1)}, u32[]{:S(2)}) copy-start(f32[4096]{0:T(1024)S(1)} %convert_element_type.150) | copy-start | bytes 49156
  199.8 26.9 %copy-start.45 = (f32[128]{0:T(128)}, f32[128]{0:T(128)S(1)}, u32[]{:S(2)}) copy-start(f32[128]{0:T(128)S(1)} %broadcast_multiply_fusion.10) | copy-start | bytes 1540
  200.8 25.9 %copy-start.49 = (f32[128]{0:T(128)}, f32[128]{0:T(128)S(1)}, u32[]{:S(2)}) copy-start(f32[128]{0:T(128)S(1)} %add_rsqrt_fusion.1) | copy-start | bytes 1540
  347.0 412.7 %reduce-scatter.16.cloned.1.call-start = ((), (), s32[]{:S(2)}) async-start(), calls=%async_computation.14 | async-start | bytes 3145728 | tf_op jit(solution)/shard_map/reduce_scatter | solution.py:274
  349.9 409.8 %reduce-scatter.18.cloned.1.call-start = ((), (), s32[]{:S(2)}) async-start(), calls=%async_computation.15 | async-start | bytes 12582912 | tf_op jit(solution)/shard_map/reduce_scatter | solution.py:277
  356.3 403.4 %reduce-scatter.20.cloned.1.call-start = ((), (), s32[]{:S(2)}) async-start(), calls=%async_computation.16 | async-start | bytes 12582912 | tf_op jit(solution)/shard_map/reduce_scatter | solution.py:280
  364.1 401.0 %reduce-scatter.24.cloned.1.call-start = ((), (), s32[]{:S(2)}) async-start(), calls=%async_computation.18 | async-start | bytes 393216
  364.1 36.7 %copy-start.42 = (bf16[1024]{0:T(1024)(128)(2,1)S(1)}, bf16[1024]{0:T(1024)(128)(2,1)}, u32[]{:S(2)}) copy-start(bf16[1024]{0:T(1024)(128)(2,1)} %get-tuple-element.772) | copy-start | bytes 6148
  364.1 36.7 %copy-start.57 = (bf16[1024]{0:T(1024)(128)(2,1)S(1)}, bf16[1024]{0:T(1024)(128)(2,1)}, u32[]{:S(2)}) copy-start(bf16[1024]{0:T(1024)(128)(2,1)} %get-tuple-element.770) | copy-start | bytes 6148
  364.1 36.7 %copy-start.41 = (bf16[1024]{0:T(1024)(128)(2,1)S(1)}, bf16[1024]{0:T(1024)(128)(2,1)}, u32[]{:S(2)}) copy-start(bf16[1024]{0:T(1024)(128)(2,1)} %get-tuple-element.753) | copy-start | bytes 6148
  364.2 36.8 %copy-start.56 = (bf16[1024]{0:T(1024)(128)(2,1)S(1)}, bf16[1024]{0:T(1024)(128)(2,1)}, u32[]{:S(2)}) copy-start(bf16[1024]{0:T(1024)(128)(2,1)} %get-tuple-element.769) | copy-start | bytes 6148
  400.6 301.2 %copy-start.5 = (bf16[1,128,1024]{2,1,0:T(8,128)(2,1)S(1)}, bf16[1,128,1024]{2,1,0:T(8,128)(2,1)}, u32[]{:S(2)}) copy-start(bf16[1,128,1024]{2,1,0:T(8,128)(2,1)} %param.18) | copy-start | bytes 786436
  400.6 301.2 %copy-start.24 = (f32[1,1024]{1,0:T(1,128)S(1)}, f32[1,1024]{1,0:T(1,128)}, u32[]{:S(2)}) copy-start(f32[1,1024]{1,0:T(1,128)} %copy-done.23) | copy-start | bytes 12292
  400.6 301.2 %copy-start.36 = (f32[128]{0:T(128)S(1)}, f32[128]{0:T(128)}, u32[]{:S(2)}) copy-start(f32[128]{0:T(128)} %copy-done.35) | copy-start | bytes 1540
  400.6 301.2 %copy-start.38 = (f32[128]{0:T(128)S(1)}, f32[128]{0:T(128)}, u32[]{:S(2)}) copy-start(f32[128]{0:T(128)} %copy-done.37) | copy-start | bytes 1540
  707.9 68.8 %reduce-scatter.22.cloned.1.call-start = ((), (), s32[]{:S(2)}) async-start(), calls=%async_computation.17 | async-start | bytes 393216
  708.9 86.7 %reduce-scatter.14.cloned.1.call-start = ((), (), s32[]{:S(2)}) async-start(), calls=%async_computation.13 | async-start | bytes 9437184 | tf_op jit(solution)/shard_map/reduce_scatter | solution.py:271
  713.6 42.1 %copy-start.39 = (bf16[4096]{0:T(1024)(128)(2,1)S(1)}, bf16[4096]{0:T(1024)(128)(2,1)}, u32[]{:S(2)}) copy-start(bf16[4096]{0:T(1024)(128)(2,1)} %get-tuple-element.749) | copy-start | bytes 24580
  713.6 42.1 %copy-start.40 = (bf16[4096]{0:T(1024)(128)(2,1)S(1)}, bf16[4096]{0:T(1024)(128)(2,1)}, u32[]{:S(2)}) copy-start(bf16[4096]{0:T(1024)(128)(2,1)} %get-tuple-element.752) | copy-start | bytes 24580
  713.6 42.1 %copy-start.55 = (bf16[16]{0:T(256)(128)(2,1)S(1)}, bf16[16]{0:T(256)(128)(2,1)}, u32[]{:S(2)}) copy-start(bf16[16]{0:T(256)(128)(2,1)} %get-tuple-element.759) | copy-start | bytes 100
  713.6 46.1 %copy-start.13 = (f32[128,1024]{1,0:T(8,128)S(1)}, f32[128,1024]{1,0:T(8,128)}, u32[]{:S(2)}) copy-start(f32[128,1024]{1,0:T(8,128)} %copy-done.12) | copy-start | bytes 1572868
  759.7 35.9 %copy-start.22 = (bf16[512,1024]{1,0:T(8,128)(2,1)S(1)}, bf16[512,1024]{1,0:T(8,128)(2,1)}, u32[]{:S(2)}) copy-start(bf16[512,1024]{1,0:T(8,128)(2,1)} %reduce-scatter.16.cloned.1.call-done) | copy-start | bytes 3145732
  (44 other events, 228.0 us)
Sparse Core Ops, SparseCore 0:
  9.6 17.9 all-gather.5
  32.5 111.1 all-gather.7
  145.2 11.0 all-gather.9
  157.7 21.0 all-gather.11
  180.1 21.0 all-gather.13
  347.0 353.4 reduce-scatter.11
  703.3 10.1 reduce-scatter.15
  716.4 17.6 reduce-scatter.17
  736.3 17.6 reduce-scatter.19
  756.1 8.8 reduce-scatter.23
  767.8 8.8 reduce-scatter.21
  779.4 16.0 reduce-scatter.13
where the time goes:
time: 1870 us
  blocking collectives  1120 us (60%)
  waiting for transfers between devices  451 us (24%)
  matrix products  136 us (7%)
  local copies, waits for them, and re-layouts  102 us (5%)
  other arithmetic  38.7 us (2%)
    psum x1, blocking collectives, local(): lax.psum((shard_grads[0], shard_grads[1], shard_grads[2], shard_grads[3],...  1070 us
    reduce_scatter x1, waiting for transfers between devices, local(): lax.psum_scatter(lax.map(key_term, sub_firsts).reshape(n_rows, 2 * model_...  300 us
    all_gather x1, waiting for transfers between devices, local(): fetched = lax.all_gather(keys_values, 'ctx', axis=0, tiled=True)  101 us
    psum x1, blocking collectives, local(): lax.psum(jnp.stack([jnp.sum(result * result), jnp.sum(attn_out * attn_out...  38.6 us
  transfers between devices with their start and end apart: 12, of which 6 were waited for; matrix products, arithmetic and copies ran while one was open for 7% of the time, Pallas kernels for 0%

commit v1 on v0

--- a/solution.py
+++ b/solution.py
@@ -9,6 +9,12 @@
 HEAD_DIM = 64
 epsilon = 1e-05
 masked_value = -1e30
+
+
+def add_all(x, name):
+    parts = lax.all_gather(x, name, axis=0, tiled=False)
+    total = parts.sum(axis=0)
+    return total
 
 
 def stored_positions(first_row, n_rows, half_rows, groups):
@@ -173,7 +179,7 @@
     mixed_in = (norm_mid * mid_gains + mid_biases).astype(jnp.bfloat16)
     ffn_out = jnp.dot(mixed_in, fc2_full, preferred_element_type=jnp.float32)
     result = middle + ffn_out
-    sq_sums = lax.psum(
+    sq_sums = add_all(
         jnp.stack(
             [jnp.sum(result * result), jnp.sum(attn_out * attn_out), jnp.sum(ffn_out * ffn_out)]
         ),

time: 1870 us -> 1870 us (level)
    psum x1 -> x0, blocking collectives: 38.6 us -> none  [local(): lax.psum(jnp.stack([jnp.sum(result * result), jnp.sum(attn_out * attn_out...]
    unnamed x2 -> x3, blocking collectives: 5.84 us -> 44.4 us
where the time goes in v1:
time: 1870 us
  blocking collectives  1120 us (60%)
  waiting for transfers between devices  451 us (24%)
  matrix products  136 us (7%)
  local copies, waits for them, and re-layouts  102 us (5%)
  other arithmetic  38.8 us (2%)
    psum x1, blocking collectives, local(): lax.psum((shard_grads[0], shard_grads[1], shard_grads[2], shard_grads[3],...  1070 us
    reduce_scatter x1, waiting for transfers between devices, local(): lax.psum_scatter(lax.map(key_term, sub_firsts).reshape(n_rows, 2 * model_...  300 us
    all_gather x1, waiting for transfers between devices, local(): fetched = lax.all_gather(keys_values, 'ctx', axis=0, tiled=True)  101 us
    unnamed x3, blocking collectives  44.4 us
  transfers between devices with their start and end apart: 12, of which 6 were waited for; matrix products, arithmetic and copies ran while one was open for 7% of the time, Pallas kernels for 0%

profile of v1, /device:TPU:26, one launch (start us, length us, event | category | flops | bytes accessed | tf_op | source)
XLA Modules:
  0.0 1870.3 jit_solution(6255520606601220638)
XLA Ops:
  12.1 15.5 all-gather.7.cloned.1.call-done
  43.0 100.6 %all-gather.9.cloned.1.call-done = bf16[2048,2048]{1,0:T(8,128)(2,1)} async-done(((bf16[128,2048]{1,0:T(8,128)(2,1)}), bf16[2048,2048]{1,0:T(8,128)(2,1)}) %all-gather.9.cloned.1.call-update) | async-done | bytes 8388624 | tf_op jit(solution)/shard_map/all_gather | solution.py:135
  143.6 12.0 copy.75
  155.7 40.6 %while.47 = (s32[]{:T(128)}, f32[128,16,64]{0,2,1:T(8,128)S(1)}, f32[128,16]{0,1:T(8,128)S(1)}, f32[128,16]{0,1:T(8,128)S(1)}, s32[2]{0:T(128)S(1)}, /*index=5*/...) while((s32[]{:T(128)}, f32[128,16,64]{0,2,1:T(8,128)S(1)}, ...), condition=%wide.region_7.8_spmd.clone, body=%wide.region_4.7_spmd.clone.sunk | while | flops 560786944 | bytes 81667752 | solution.py:163
  165.5 6.6 fusion.229
  185.8 6.3 fusion.229
  200.8 5.5 fusion.131
  207.5 6.7 multiply_reduce_fusion
  216.3 6.7 fusion.143
  230.1 116.8 %while.46 = (s32[]{:T(128)}, f32[2,1024,2048]{2,1,0:T(8,128)}, s32[2]{0:T(128)S(1)}, s32[128]{0:T(128)S(1)}, bf16[2048,2048]{1,0:T(8,128)(2,1)}, /*index=5*/bf16...) while((s32[]{:T(128)}, f32[2,1024,2048]{2,1,0:T(8,128)}, ...), condition=%wide.region_24.25_spmd.clone, body=%wide.region_23.24_spmd.clone.sunk | while | flops 1098302976 | bytes 123111664 | solution.py:263
  233.2 5.3 fusion.216
  242.4 6.3 fusion.217
  252.3 10.0 broadcast_multiply_fusion.14
  262.2 5.4 fusion.220
  271.9 9.1 copy.130
  281.0 7.7 constant_dynamic-update-slice_fusion.2
  291.4 5.3 fusion.216
  300.6 6.3 fusion.217
  310.5 10.0 broadcast_multiply_fusion.14
  320.4 5.4 fusion.220
  330.1 9.1 copy.130
  339.2 7.7 constant_dynamic-update-slice_fusion.2
  350.2 6.0 convolution_convert_fusion.1
  357.9 6.2 convolution_convert_fusion
  364.2 36.4 %while.48 = (s32[]{:T(128)}, f32[128,16,64]{0,2,1:T(8,128)S(1)}, bf16[2,1024,2048]{1,2,0:T(8,128)(2,1)}, s32[2]{0:T(128)S(1)}, s32[128]{0:T(128)S(1)}, /*index=5...) while((s32[]{:T(128)}, f32[128,16,64]{0,2,1:T(8,128)S(1)}, ...), condition=%wide.region_22.23_spmd.clone, body=%wide.region_21.22_spmd.clone.sunk | while | flops 818595328 | bytes 41707156 | solution.py:234
  374.6 7.8 fusion.242
  392.9 7.7 fusion.242
  400.9 299.6 %reduce-scatter.12.cloned.1.call-done = f32[128,2048]{1,0:T(8,128)} async-done(((f32[2048,2048]{1,0:T(8,128)}), f32[128,2048]{1,0:T(8,128)}) %reduce-scatter.12.cloned.1.call-update) | async-done | bytes 1048592 | tf_op jit(solution)/shard_map/reduce_scatter | solution.py:262
  717.1 38.6 %all-reduce.1 = f32[96]{0:T(128)S(1)} all-reduce(f32[96]{0:T(128)S(1)} %maximum_dynamic-update-slice_fusion), channel_id=2, replica_groups=mesh['ctx'=16,'fsdp'=2] {'ctx','fsdp'}, use_global_device_ids=true, to_apply=%add.1 | all-reduce | flops 96 | bytes 768
  766.0 10.7 reduce-scatter.22.cloned.1.call-done
  777.7 17.9 reduce-scatter.14.cloned.1.call-done
  795.6 1067.7 %all-reduce.8 = (f32[512,3072]{1,0:T(8,128)}, f32[512,1024]{1,0:T(8,128)}, f32[512,4096]{1,0:T(8,128)}, f32[2048,1024]{1,0:T(8,128)}, f32[3,512]{1,0:T(4,128)}, ...) all-reduce(bf16[512,3072]{1,0:T(8,128)(2,1)} %reduce-scatter.14.clo, ...), channel_id=1, replica_groups=mesh['ctx'=16,'fsdp'=2] {'ctx'}, use_global_device_ids=true, to_apply=%region_29.30 | all-reduce | flops 6298632 | bytes 37800000 | tf_op jit(solution)/shard_map/psum | solution.py:305
  (294 shorter events, 138.4 us)
Async XLA Ops:
  7.2 20.4 %all-gather.7.cloned.1.call-start = ((), (), s32[]{:S(2)}) async-start(), calls=%async_computation.7 | async-start | bytes 9437184 | tf_op jit(solution)/shard_map/all_gather | solution.py:105
  7.9 135.7 %all-gather.9.cloned.1.call-start = ((), (), s32[]{:S(2)}) async-start(), calls=%async_computation.8 | async-start | bytes 8912896 | tf_op jit(solution)/shard_map/all_gather | solution.py:135
  11.8 19.7 %copy-start.35 = (f32[128]{0:T(128)}, f32[128]{0:T(128)S(1)}, u32[]{:S(2)}) copy-start(f32[128]{0:T(128)S(1)} %broadcast_multiply_fusion.12) | copy-start | bytes 1540
  12.0 214.6 %copy-start.29 = (f32[1,1024]{1,0:T(1,128)}, f32[1,1024]{1,0:T(1,128)S(1)}, u32[]{:S(2)}) copy-start(f32[1,1024]{1,0:T(1,128)S(1)} %get-tuple-element.858) | copy-start | bytes 12292
  12.1 188.7 %copy-start.33 = (f32[1,1024]{1,0:T(1,128)}, f32[1,1024]{1,0:T(1,128)S(1)}, u32[]{:S(2)}) copy-start(f32[1,1024]{1,0:T(1,128)S(1)} %get-tuple-element.861) | copy-start | bytes 12292
  32.3 164.1 %all-gather.11.cloned.1.call-start = ((), (), s32[]{:S(2)}) async-start(), calls=%async_computation.9 | async-start | bytes 3145728 | tf_op jit(solution)/shard_map/all_gather | solution.py:106
  33.1 167.7 %all-gather.13.cloned.1.call-start = ((), (), s32[]{:S(2)}) async-start(), calls=%async_computation.10 | async-start | bytes 12582912 | tf_op jit(solution)/shard_map/all_gather | solution.py:107
  33.7 173.6 %all-gather.15.cloned.1.call-start = ((), (), s32[]{:S(2)}) async-start(), calls=%async_computation.11 | async-start | bytes 12582912 | tf_op jit(solution)/shard_map/all_gather | solution.py:108
  34.3 666.2 %reduce-scatter.12.cloned.1.call-start = ((), (), s32[]{:S(2)}) async-start(), calls=%async_computation.12 | async-start | bytes 17825792 | tf_op jit(solution)/shard_map/reduce_scatter | solution.py:262
  40.4 182.7 %copy-start.27 = (f32[4096]{0:T(1024)}, f32[4096]{0:T(1024)S(1)}, u32[]{:S(2)}) copy-start(f32[4096]{0:T(1024)S(1)} %convert_element_type.149) | copy-start | bytes 49156
  42.7 180.4 %copy-start.31 = (f32[4096]{0:T(1024)}, f32[4096]{0:T(1024)S(1)}, u32[]{:S(2)}) copy-start(f32[4096]{0:T(1024)S(1)} %convert_element_type.150) | copy-start | bytes 49156
  199.8 26.9 %copy-start.45 = (f32[128]{0:T(128)}, f32[128]{0:T(128)S(1)}, u32[]{:S(2)}) copy-start(f32[128]{0:T(128)S(1)} %broadcast_multiply_fusion.10) | copy-start | bytes 1540
  200.8 25.9 %copy-start.49 = (f32[128]{0:T(128)}, f32[128]{0:T(128)S(1)}, u32[]{:S(2)}) copy-start(f32[128]{0:T(128)S(1)} %add_rsqrt_fusion.1) | copy-start | bytes 1540
  347.0 412.9 %reduce-scatter.16.cloned.1.call-start = ((), (), s32[]{:S(2)}) async-start(), calls=%async_computation.14 | async-start | bytes 3145728 | tf_op jit(solution)/shard_map/reduce_scatter | solution.py:280
  349.9 409.9 %reduce-scatter.18.cloned.1.call-start = ((), (), s32[]{:S(2)}) async-start(), calls=%async_computation.15 | async-start | bytes 12582912 | tf_op jit(solution)/shard_map/reduce_scatter | solution.py:283
  356.3 403.6 %reduce-scatter.20.cloned.1.call-start = ((), (), s32[]{:S(2)}) async-start(), calls=%async_computation.16 | async-start | bytes 12582912 | tf_op jit(solution)/shard_map/reduce_scatter | solution.py:286
  364.1 401.0 %reduce-scatter.24.cloned.1.call-start = ((), (), s32[]{:S(2)}) async-start(), calls=%async_computation.18 | async-start | bytes 393216
  364.1 36.7 %copy-start.42 = (bf16[1024]{0:T(1024)(128)(2,1)S(1)}, bf16[1024]{0:T(1024)(128)(2,1)}, u32[]{:S(2)}) copy-start(bf16[1024]{0:T(1024)(128)(2,1)} %get-tuple-element.772) | copy-start | bytes 6148
  364.1 36.7 %copy-start.57 = (bf16[1024]{0:T(1024)(128)(2,1)S(1)}, bf16[1024]{0:T(1024)(128)(2,1)}, u32[]{:S(2)}) copy-start(bf16[1024]{0:T(1024)(128)(2,1)} %get-tuple-element.770) | copy-start | bytes 6148
  364.1 36.7 %copy-start.41 = (bf16[1024]{0:T(1024)(128)(2,1)S(1)}, bf16[1024]{0:T(1024)(128)(2,1)}, u32[]{:S(2)}) copy-start(bf16[1024]{0:T(1024)(128)(2,1)} %get-tuple-element.753) | copy-start | bytes 6148
  364.2 36.8 %copy-start.56 = (bf16[1024]{0:T(1024)(128)(2,1)S(1)}, bf16[1024]{0:T(1024)(128)(2,1)}, u32[]{:S(2)}) copy-start(bf16[1024]{0:T(1024)(128)(2,1)} %get-tuple-element.769) | copy-start | bytes 6148
  400.6 301.2 %copy-start.5 = (bf16[1,128,1024]{2,1,0:T(8,128)(2,1)S(1)}, bf16[1,128,1024]{2,1,0:T(8,128)(2,1)}, u32[]{:S(2)}) copy-start(bf16[1,128,1024]{2,1,0:T(8,128)(2,1)} %param.18) | copy-start | bytes 786436
  400.6 301.2 %copy-start.24 = (f32[1,1024]{1,0:T(1,128)S(1)}, f32[1,1024]{1,0:T(1,128)}, u32[]{:S(2)}) copy-start(f32[1,1024]{1,0:T(1,128)} %copy-done.23) | copy-start | bytes 12292
  400.6 301.2 %copy-start.36 = (f32[128]{0:T(128)S(1)}, f32[128]{0:T(128)}, u32[]{:S(2)}) copy-start(f32[128]{0:T(128)} %copy-done.35) | copy-start | bytes 1540
  400.6 301.2 %copy-start.38 = (f32[128]{0:T(128)S(1)}, f32[128]{0:T(128)}, u32[]{:S(2)}) copy-start(f32[128]{0:T(128)} %copy-done.37) | copy-start | bytes 1540
  707.9 68.8 %reduce-scatter.22.cloned.1.call-start = ((), (), s32[]{:S(2)}) async-start(), calls=%async_computation.17 | async-start | bytes 393216
  708.9 86.7 %reduce-scatter.14.cloned.1.call-start = ((), (), s32[]{:S(2)}) async-start(), calls=%async_computation.13 | async-start | bytes 9437184 | tf_op jit(solution)/shard_map/reduce_scatter | solution.py:277
  713.6 42.2 %copy-start.39 = (bf16[4096]{0:T(1024)(128)(2,1)S(1)}, bf16[4096]{0:T(1024)(128)(2,1)}, u32[]{:S(2)}) copy-start(bf16[4096]{0:T(1024)(128)(2,1)} %get-tuple-element.749) | copy-start | bytes 24580
  713.6 42.2 %copy-start.40 = (bf16[4096]{0:T(1024)(128)(2,1)S(1)}, bf16[4096]{0:T(1024)(128)(2,1)}, u32[]{:S(2)}) copy-start(bf16[4096]{0:T(1024)(128)(2,1)} %get-tuple-element.752) | copy-start | bytes 24580
  713.6 42.2 %copy-start.55 = (bf16[16]{0:T(256)(128)(2,1)S(1)}, bf16[16]{0:T(256)(128)(2,1)}, u32[]{:S(2)}) copy-start(bf16[16]{0:T(256)(128)(2,1)} %get-tuple-element.759) | copy-start | bytes 100
  713.6 46.3 %copy-start.13 = (f32[128,1024]{1,0:T(8,128)S(1)}, f32[128,1024]{1,0:T(8,128)}, u32[]{:S(2)}) copy-start(f32[128,1024]{1,0:T(8,128)} %copy-done.12) | copy-start | bytes 1572868
  759.9 35.7 %copy-start.22 = (bf16[512,1024]{1,0:T(8,128)(2,1)S(1)}, bf16[512,1024]{1,0:T(8,128)(2,1)}, u32[]{:S(2)}) copy-start(bf16[512,1024]{1,0:T(8,128)(2,1)} %reduce-scatter.16.cloned.1.call-done) | copy-start | bytes 3145732
  (44 other events, 228.0 us)
Sparse Core Ops, SparseCore 0:
  9.6 17.9 all-gather.6
  32.5 111.1 all-gather.8
  145.2 11.0 all-gather.10
  157.7 21.0 all-gather.12
  180.1 21.0 all-gather.14
  347.0 353.4 reduce-scatter.11
  703.3 10.1 reduce-scatter.15
  716.4 17.6 reduce-scatter.17
  736.3 17.6 reduce-scatter.19
  756.1 8.8 reduce-scatter.23
  767.8 8.8 reduce-scatter.21
  779.4 16.0 reduce-scatter.13
